TPU v7x, 32 devices: a whole 2x2x4 slice. The times are simulated.
32 devices in a mesh: groups: 2 (over y), space: 4 (over z), clus: 4 (over x, core).
Axes of the slice: x: 2, y: 2, z: 4, core: 2. Of those that a mesh axis runs over, the one named last changes fastest.
Arguments:
- snapshots: bfloat16 [256, 5, 49152], P('groups', None, ('space', 'clus')), parts along dimension 0
- labels: int32 [256], P('groups'), parts along dimension 0, may hold values from 0 to 3, as said below
- start: float32 [256, 16], P('groups'), parts along dimension 0, may hold values from -6 to 6
- successor: int32 [8], P('groups'), parts along dimension 0, may hold values from 0 to 3, as said below
Outputs:
- modes: bfloat16 [8, 16, 5, 49152], P(('groups', 'clus'), None, None, 'space'), parts along dimension 0
- coefficients: float32 [256, 16], P(('groups', 'clus')), parts along dimension 0
- correlations: float32 [8, 16, 16], P(('groups', 'clus')), parts along dimension 0
There are 2 independent parts, one for each index of `groups`. A program takes and returns all parts, laid end to end along the dimension named above; each array names one. Nothing has to cross between parts.
Inputs may be any that keep to these rules, and one draw needn't show every extreme that they name: `labels`: of the 32 snapshots of each aligned block (those of one index of clus), every cluster holds at least 6 and at most 8; in every block some cluster holds exactly 8. Following successor from any cluster visits all 4 clusters once before returning.
All inputs are finite; a program needn't handle non-finite values.
Results may differ from a plain program's by a relative error of at most 0.0045.
Values may be sent and summed in bfloat16 or wider, within the bound.
No kernel may reach another device: no remote copies, remote signals or barrier semaphores. Data moves between devices by JAX's collectives and lax.ppermute only.
A program may use at most 64 MiB of HBM per device.

v0:
```python
import jax
import jax.numpy as jnp
from jax import lax
from jax.sharding import PartitionSpec as P

ITERS = 2


def subspace(gram, member, start):
    basis = member[:, :, None] * start[None, :, :]
    for step in range(ITERS):
        image = (
            member[:, :, None]
            * jnp.einsum("st,ktm->ksm", gram, basis, precision=lax.Precision.HIGHEST)
            + basis
        )
        inner = jnp.einsum("ksm,ksn->kmn", image, image, precision=lax.Precision.HIGHEST)
        lower = jnp.linalg.cholesky(inner)
        basis = lax.linalg.triangular_solve(
            lower, image, left_side=False, lower=True, transpose_a=True
        )
    return basis


def local(snapshots, labels, start, successor):
    count, variables, cells = snapshots.shape
    clusters = lax.axis_size("clus")
    owner = lax.axis_index("clus")
    total_rows = variables * cells * lax.axis_size("space") * clusters
    flat = snapshots.reshape(count, variables * cells)
    partial_value = lax.dot_general(
        flat, flat, (((1,), (1,)), ((), ())), preferred_element_type=jnp.float32
    )
    gram = lax.psum(partial_value, ("space", "clus")) / total_rows
    cluster_ids = jnp.arange(clusters, dtype=jnp.int32)
    member = (labels[None, :] == cluster_ids[:, None]).astype(jnp.float32)
    basis = subspace(gram, member, start)
    picked = jnp.einsum("ks,ksm->sm", member, basis, precision=lax.Precision.HIGHEST)
    snap_dev = count // clusters
    coefficients = lax.dynamic_slice_in_dim(picked, owner * snap_dev, snap_dev, 0)
    rounded = basis.astype(jnp.bfloat16)
    mode_count = rounded.shape[2]
    modes_full = None
    left = jnp.transpose(rounded, (0, 2, 1)).reshape(clusters * mode_count, count)
    modes_full = jnp.dot(left, flat, preferred_element_type=jnp.float32)
    packed = modes_full.astype(jnp.bfloat16).reshape(clusters, mode_count, variables, cells)
    modes_out = lax.all_to_all(packed, "clus", split_axis=0, concat_axis=3, tiled=True)
    select = (successor[:, None] == cluster_ids[None, :]).astype(jnp.float32)
    wide = rounded.astype(jnp.float32)
    partner = jnp.einsum("ab,bsn->asn", select, wide, precision=lax.Precision.HIGHEST)
    image = jnp.einsum("st,atn->asn", gram, partner, precision=lax.Precision.HIGHEST)
    correlations = jnp.einsum("asm,asn->amn", wide, image, precision=lax.Precision.HIGHEST)
    own_correlation = lax.dynamic_slice_in_dim(correlations, owner, 1, 0)
    return (modes_out, coefficients, own_correlation)


def solution(mesh):
    in_specs = (P("groups", None, ("space", "clus")), P("groups"), P("groups", None), P("groups"))
    out_specs = (
        P(("groups", "clus"), None, None, "space"),
        P(("groups", "clus"), None),
        P(("groups", "clus"), None, None),
    )
    return jax.shard_map(local, mesh=mesh, in_specs=in_specs, out_specs=out_specs, check_vma=False)
```

profile of v0, /device:TPU:8, one launch (start us, length us, event | category | flops | bytes accessed | tf_op | source)
XLA Modules:
  0.0 174.2 jit_solution(173776694287602055)
XLA Ops:
  7.2 0.0 all-reduce.2.cloned.1.call-start
  7.2 5.1 %convolution_bitcast_fusion = f32[128,128]{1,0:T(8,128)} fusion(bf16[128,5,3072]{2,0,1:T(8,128)(2,1)} %param.7), kind=kOutput, calls=%fused_computation.1 | convolution fusion | flops 503316480 | bytes 3997696 | tf_op jit(solution)/shard_map/dot_general | solution.py:31
  12.4 0.0 all-reduce.2.cloned.1.call-update
  12.4 6.3 %copy.38 = bf16[128,5,3072]{0,2,1:T(8,128)(2,1)} copy(bf16[128,5,3072]{2,0,1:T(8,128)(2,1)} %param.7) | data formatting | bytes 7864320 | tf_op args[0]
  18.7 82.0 %all-reduce.2.cloned.1.call-done = f32[128,128]{1,0:T(8,128)} async-done(((f32[128,128]{1,0:T(8,128)}), f32[128,128]{1,0:T(8,128)}) %all-reduce.2.cloned.1.call-update) | async-done | bytes 65552 | tf_op jit(solution)/shard_map/psum | solution.py:34
  100.7 1.1 fusion.3
  101.8 0.2 fusion.35
  102.0 0.1 copy.34
  102.1 5.9 %custom-call.8 = f32[4,16,16]{2,1,0:T(8,128)S(1)} custom-call(f32[4,16,16]{2,1,0:T(8,128)S(1)} %fusion.16), custom_call_target="Cholesky" | custom-call | tf_op jit(solution)/shard_map/jit(cholesky)/cholesky | solution.py:18
  108.0 0.1 compare_reduce_fusion.1
  108.1 0.1 select_bitcast_fusion.1
  108.2 4.9 %custom-call.9 = f32[4,1,16,16]{2,3,1,0:T(8,128)S(1)} custom-call(f32[4,1,16,16]{3,2,1,0:T(8,128)S(1)} %select_bitcast_fusion.1), custom_call_target="InvertDiagBlocksLowerTriangular" | custom-call | tf_op jit(solution)/shard_map/triangular_solve/custom-call.0 | solution.py:19
  113.1 0.3 convolution_bitcast_fusion.1
  113.4 1.1 fusion.1
  114.5 0.2 fusion.36
  114.6 0.1 copy.36
  114.7 5.9 %custom-call.10 = f32[4,16,16]{2,1,0:T(8,128)S(1)} custom-call(f32[4,16,16]{2,1,0:T(8,128)S(1)} %fusion.14), custom_call_target="Cholesky" | custom-call | tf_op jit(solution)/shard_map/jit(cholesky)/cholesky | solution.py:18
  120.6 0.1 compare_reduce_fusion
  120.7 0.1 select_bitcast_fusion
  120.8 4.9 %custom-call.11 = f32[4,1,16,16]{2,3,1,0:T(8,128)S(1)} custom-call(f32[4,1,16,16]{3,2,1,0:T(8,128)S(1)} %select_bitcast_fusion), custom_call_target="InvertDiagBlocksLowerTriangular" | custom-call | tf_op jit(solution)/shard_map/triangular_solve/custom-call.0 | solution.py:19
  125.7 0.3 bitcast_convert_fusion
  126.0 4.9 %convolution_convert_fusion = bf16[64,15360]{1,0:T(8,128)(2,1)} fusion(bf16[64,128]{1,0:T(8,128)(2,1)S(1)} %bitcast.78, bf16[128,15360]{0,1:T(8,128)(2,1)} %bitcast.75), kind=kOutput, calls=%fused_computation | convolution fusion | flops 252641280 | bytes 5914624 | tf_op jit(solution)/shard_map/dot_general | solution.py:45
  130.9 4.6 %reshape.50 = bf16[4,16,5,3072]{3,2,1,0:T(8,128)(2,1)S(1)} reshape(bf16[64,15360]{1,0:T(8,128)(2,1)} %convolution_convert_fusion) | data formatting | bytes 3932160 | tf_op jit(solution)/shard_map/reshape | solution.py:46
  135.5 2.6 %copy.39 = bf16[4,16,5,3072]{3,1,2,0:T(8,128)(2,1)} copy(bf16[4,16,5,3072]{3,2,1,0:T(8,128)(2,1)S(1)} %reshape.50) | data formatting | bytes 3932160 | tf_op jit(solution)/shard_map/reshape | solution.py:46
  138.1 3.6 %all-to-all-start = ((bf16[4,16,5,3072]{3,1,2,0:T(8,128)(2,1)}), bf16[4,16,5,3072]{3,1,2,0:T(8,128)(2,1)S(1)}, u32[]{:S(2)}, u32[]{:S(2)}) async-start(bf16[4,16,5,3072]{3,1,2,0:T(8,128)(2,1)} %copy.39), calls=%async_computation | async-start | bytes 3932160 | tf_op jit(solution)/shard_map/all_to_all | solution.py:47
  141.7 0.7 constant_dynamic-slice_fusion.1
  142.4 0.2 fusion.22
  142.6 0.2 fusion.4
  142.8 0.1 fusion.37
  143.0 0.6 constant_dynamic-slice_fusion
  143.6 22.4 %all-to-all-done = bf16[4,16,5,3072]{3,1,2,0:T(8,128)(2,1)S(1)} async-done(((bf16[4,16,5,3072]{3,1,2,0:T(8,128)(2,1)}), bf16[4,16,5,3072]{3,1,2,0:T(8,128)(2,1)S(1)}, u32[]{:S(2)}, u32[]{:S(2)}) %all-to-all-start) | async-done | bytes 1966112 | tf_op jit(solution)/shard_map/all_to_all | solution.py:47
  165.9 1.4 copy.52
  (16 shorter events, 0.1 us)
Async XLA Ops:
  7.2 5.2 %copy-start.2 = (s32[128]{0:T(128)S(1)}, s32[128]{0:T(128)}, u32[]{:S(2)}) copy-start(s32[128]{0:T(128)} %param.8) | copy-start | bytes 1540
  7.2 93.5 %all-reduce.2.cloned.1.call-start = ((), (), s32[]{:S(2)}) async-start(), calls=%async_computation.1 | async-start | bytes 131072 | tf_op jit(solution)/shard_map/psum | solution.py:34
  12.4 88.3 %copy-start.1 = (f32[128,16]{0,1:T(8,128)S(1)}, f32[128,16]{0,1:T(8,128)}, u32[]{:S(2)}) copy-start(f32[128,16]{0,1:T(8,128)} %param.9) | copy-start | bytes 24580
  135.5 6.9 %copy-start.3 = (s32[4]{0:T(128)S(1)}, s32[4]{0:T(128)}, u32[]{:S(2)}) copy-start(s32[4]{0:T(128)} %param.10) | copy-start | bytes 52
  135.5 7.1 %copy-start = (f32[128,128]{1,0:T(8,128)S(1)}, f32[128,128]{1,0:T(8,128)}, u32[]{:S(2)}) copy-start(f32[128,128]{1,0:T(8,128)} %all-reduce.2.cloned.1.call-done) | copy-start | bytes 196612
  138.1 27.9 %all-to-all-start = ((bf16[4,16,5,3072]{3,1,2,0:T(8,128)(2,1)}), bf16[4,16,5,3072]{3,1,2,0:T(8,128)(2,1)S(1)}, u32[]{:S(2)}, u32[]{:S(2)}) async-start(bf16[4,16,5,3072]{3,1,2,0:T(8,128)(2,1)} %copy.39), calls=%async_computation | async-start | bytes 3932160 | tf_op jit(solution)/shard_map/all_to_all | solution.py:47
Sparse Core Ops, SparseCore 0:
  12.5 88.1 all-reduce.1
where the time goes:
time: 175 us; the launch traced here: 174 us
  waiting for transfers between devices  104 us (59%)
  other arithmetic  22.1 us (13%)
  local copies, waits for them, and re-layouts  16.3 us (9%)
  between operations  14.2 us (8%)
  matrix products  13.6 us (8%)
  starting transfers between devices  3.64 us (2%)
    psum x1, waiting for transfers between devices, local(): gram = lax.psum(partial_value, ('space', 'clus')) / total_rows  82 us
    all_to_all x1, waiting for transfers between devices, local(): lax.all_to_all(packed, 'clus', split_axis=0, concat_axis=3, tiled=True)  22.4 us
    another operation x7, other arithmetic, subspace(): lower = jnp.linalg.cholesky(inner)  12 us
    another operation x5, other arithmetic, subspace(): lax.linalg.triangular_solve(lower, image, left_side=False, lower=True, tr...  9.99 us
    reshape x2, local copies, waits for them, and re-layouts, local(): modes_full.astype(jnp.bfloat16)  7.12 us
    unnamed x9, local copies, waits for them, and re-layouts  6.29 us
    dot_general x1, matrix products, local(): lax.dot_general(flat, flat, (((1,), (1,)), ((), ())), preferred_element_t...  5.13 us
    dot_general x1, matrix products, local(): modes_full = jnp.dot(left, flat, preferred_element_type=jnp.float32)  4.86 us
  transfers between devices with their start and end apart: 2, of which 2 were waited for; matrix products, arithmetic and copies ran while one was open for 5% of the time, Pallas kernels for 0%

commit v1 on v0

--- a/solution.py
+++ b/solution.py
@@ -4,6 +4,14 @@
 from jax.sharding import PartitionSpec as P
 
 ITERS = 2
+
+
+def _fill_cube(load, ax_name):
+    part_now = lax.axis_size(ax_name)
+    g_now = jnp.split(load, part_now, 0)
+    carry_out = jnp.stack(g_now, axis=0)
+    p_next = lax.all_to_all(carry_out, axis_name=ax_name, split_axis=0, concat_axis=0)
+    return jnp.concatenate(p_next, axis=3)
 
 
 def subspace(gram, member, start):
@@ -44,7 +52,7 @@
     left = jnp.transpose(rounded, (0, 2, 1)).reshape(clusters * mode_count, count)
     modes_full = jnp.dot(left, flat, preferred_element_type=jnp.float32)
     packed = modes_full.astype(jnp.bfloat16).reshape(clusters, mode_count, variables, cells)
-    modes_out = lax.all_to_all(packed, "clus", split_axis=0, concat_axis=3, tiled=True)
+    modes_out = _fill_cube(packed, "clus")
     select = (successor[:, None] == cluster_ids[None, :]).astype(jnp.float32)
     wide = rounded.astype(jnp.float32)
     partner = jnp.einsum("ab,bsn->asn", select, wide, precision=lax.Precision.HIGHEST)

time: 175 us -> 175 us (level)
    another operation x0 -> x5, local copies, waits for them, and re-layouts: none -> 6.82 us  [_fill_cube(): carry_out = jnp.stack(g_now, axis=0)]
    reshape x2 -> x1, local copies, waits for them, and re-layouts: 7.12 us -> 1.45 us  [_fill_cube(): return jnp.concatenate(p_next, axis=3)]
where the time goes in v1:
time: 175 us
  waiting for transfers between devices  104 us (59%)
  other arithmetic  22.9 us (13%)
  local copies, waits for them, and re-layouts  16.9 us (10%)
  between operations  14.2 us (8%)
  matrix products  12.4 us (7%)
  starting transfers between devices  3.77 us (2%)
    psum x1, waiting for transfers between devices, local(): gram = lax.psum(partial_value, ('space', 'clus')) / total_rows  82 us
    all_to_all x1, waiting for transfers between devices, _fill_cube(): lax.all_to_all(carry_out, axis_name=ax_name, split_axis=0, concat_axis=0)  22.4 us
    another operation x7, other arithmetic, subspace(): lower = jnp.linalg.cholesky(inner)  12 us
    another operation x5, other arithmetic, subspace(): lax.linalg.triangular_solve(lower, image, left_side=False, lower=True, tr...  9.99 us
    another operation x5, local copies, waits for them, and re-layouts, _fill_cube(): carry_out = jnp.stack(g_now, axis=0)  6.82 us
    unnamed x9, local copies, waits for them, and re-layouts  6.28 us
    dot_general x1, matrix products, local(): lax.dot_general(flat, flat, (((1,), (1,)), ((), ())), preferred_element_t...  5.13 us
    all_to_all x1, starting transfers between devices, _fill_cube(): lax.all_to_all(carry_out, axis_name=ax_name, split_axis=0, concat_axis=0)  3.73 us
  transfers between devices with their start and end apart: 2, of which 2 were waited for; matrix products, arithmetic and copies ran while one was open for 5% of the time, Pallas kernels for 0%

profile of v1, /device:TPU:8, one launch (start us, length us, event | category | flops | bytes accessed | tf_op | source)
XLA Modules:
  0.0 174.6 jit_solution(11020978703822970467)
XLA Ops:
  7.2 5.1 %convolution_bitcast_fusion = f32[128,128]{1,0:T(8,128)} fusion(bf16[128,5,3072]{2,0,1:T(8,128)(2,1)} %param.7), kind=kOutput, calls=%fused_computation.2 | convolution fusion | flops 503316480 | bytes 3997696 | tf_op jit(solution)/shard_map/dot_general | solution.py:39
  12.4 6.3 %copy.38 = bf16[128,5,3072]{0,2,1:T(8,128)(2,1)} copy(bf16[128,5,3072]{2,0,1:T(8,128)(2,1)} %param.7) | data formatting | bytes 7864320 | tf_op args[0]
  18.7 82.0 %all-reduce.2.cloned.1.call-done = f32[128,128]{1,0:T(8,128)} async-done(((f32[128,128]{1,0:T(8,128)}), f32[128,128]{1,0:T(8,128)}) %all-reduce.2.cloned.1.call-update) | async-done | bytes 65552 | tf_op jit(solution)/shard_map/psum | solution.py:42
  100.7 1.1 fusion.3
  101.8 0.2 fusion.36
  102.1 5.9 %custom-call.8 = f32[4,16,16]{2,1,0:T(8,128)S(1)} custom-call(f32[4,16,16]{2,1,0:T(8,128)S(1)} %fusion.16), custom_call_target="Cholesky" | custom-call | tf_op jit(solution)/shard_map/jit(cholesky)/cholesky | solution.py:26
  108.0 0.1 compare_reduce_fusion.1
  108.2 4.9 %custom-call.9 = f32[4,1,16,16]{2,3,1,0:T(8,128)S(1)} custom-call(f32[4,1,16,16]{3,2,1,0:T(8,128)S(1)} %select_bitcast_fusion.1), custom_call_target="InvertDiagBlocksLowerTriangular" | custom-call | tf_op jit(solution)/shard_map/triangular_solve/custom-call.0 | solution.py:27
  113.1 0.3 convolution_bitcast_fusion.1
  113.4 1.1 fusion.1
  114.5 0.2 fusion.37
  114.7 5.9 %custom-call.10 = f32[4,16,16]{2,1,0:T(8,128)S(1)} custom-call(f32[4,16,16]{2,1,0:T(8,128)S(1)} %fusion.14), custom_call_target="Cholesky" | custom-call | tf_op jit(solution)/shard_map/jit(cholesky)/cholesky | solution.py:26
  120.6 0.1 compare_reduce_fusion
  120.7 0.1 select_bitcast_fusion
  120.8 4.9 %custom-call.11 = f32[4,1,16,16]{2,3,1,0:T(8,128)S(1)} custom-call(f32[4,1,16,16]{3,2,1,0:T(8,128)S(1)} %select_bitcast_fusion), custom_call_target="InvertDiagBlocksLowerTriangular" | custom-call | tf_op jit(solution)/shard_map/triangular_solve/custom-call.0 | solution.py:27
  125.7 0.3 bitcast_convert_fusion
  126.0 3.6 %convolution_convert_fusion = bf16[64,15360]{1,0:T(8,128)(2,1)S(1)} fusion(bf16[64,128]{1,0:T(8,128)(2,1)S(1)} %bitcast.76, bf16[128,15360]{0,1:T(8,128)(2,1)} %bitcast.73), kind=kOutput, calls=%fused_computation | convolution fusion | flops 252641280 | bytes 5914624 | tf_op jit(solution)/shard_map/dot_general | solution.py:53
  129.6 0.9 fusion.35
  130.5 0.8 stack.15
  131.4 0.8 stack.18
  132.2 0.8 stack.17
  133.0 1.8 %stack.16 = bf16[1,1,16,5,3072]{4,3,2,1,0:T(8,128)(2,1)S(1)} reshape(bf16[16,15360]{1,0:T(8,128)(2,1)} %get-tuple-element.8) | data formatting | bytes 983040 | tf_op jit(solution)/shard_map/stack | solution.py:12
  134.8 0.9 pad_maximum_fusion
  135.7 2.6 %copy.39 = bf16[4,1,16,5,3072]{4,2,3,1,0:T(8,128)(2,1)} copy(bf16[4,1,16,5,3072]{4,3,2,1,0:T(8,128)(2,1)S(1)} %pad_maximum_fusion) | data formatting | bytes 3932160 | tf_op jit(solution)/shard_map/stack | solution.py:12
  138.3 3.7 %all-to-all-start = ((bf16[4,1,16,5,3072]{4,2,3,1,0:T(8,128)(2,1)}), bf16[4,1,16,5,3072]{4,2,3,1,0:T(8,128)(2,1)S(1)}, u32[]{:S(2)}, u32[]{:S(2)}) async-start(bf16[4,1,16,5,3072]{4,2,3,1,0:T(8,128)(2,1)} %copy.39), calls=%async_computation | async-start | bytes 3932160 | tf_op jit(solution)/shard_map/all_to_all | solution.py:13
  142.0 0.7 constant_dynamic-slice_fusion.1
  142.7 0.2 fusion.22
  142.9 0.2 fusion.4
  143.2 0.1 fusion.38
  143.3 0.6 constant_dynamic-slice_fusion
  143.9 22.4 %all-to-all-done = bf16[4,1,16,5,3072]{4,2,3,1,0:T(8,128)(2,1)S(1)} async-done(((bf16[4,1,16,5,3072]{4,2,3,1,0:T(8,128)(2,1)}), bf16[4,1,16,5,3072]{4,2,3,1,0:T(8,128)(2,1)S(1)}, u32[]{:S(2)}, u32[]{:S(2)}) %all-to-all-start) | async-done | bytes 1966112 | tf_op jit(solution)/shard_map/all_to_all | solution.py:13
  166.3 1.4 copy.52
  (21 shorter events, 0.4 us)
Async XLA Ops:
  7.2 5.2 %copy-start.2 = (s32[128]{0:T(128)S(1)}, s32[128]{0:T(128)}, u32[]{:S(2)}) copy-start(s32[128]{0:T(128)} %param.8) | copy-start | bytes 1540
  7.2 93.5 %all-reduce.2.cloned.1.call-start = ((), (), s32[]{:S(2)}) async-start(), calls=%async_computation.1 | async-start | bytes 131072 | tf_op jit(solution)/shard_map/psum | solution.py:42
  12.4 88.3 %copy-start.1 = (f32[128,16]{0,1:T(8,128)S(1)}, f32[128,16]{0,1:T(8,128)}, u32[]{:S(2)}) copy-start(f32[128,16]{0,1:T(8,128)} %param.9) | copy-start | bytes 24580
  138.3 4.4 %copy-start.3 = (s32[4]{0:T(128)S(1)}, s32[4]{0:T(128)}, u32[]{:S(2)}) copy-start(s32[4]{0:T(128)} %param.10) | copy-start | bytes 52
  138.3 4.6 %copy-start = (f32[128,128]{1,0:T(8,128)S(1)}, f32[128,128]{1,0:T(8,128)}, u32[]{:S(2)}) copy-start(f32[128,128]{1,0:T(8,128)} %all-reduce.2.cloned.1.call-done) | copy-start | bytes 196612
  138.3 28.0 %all-to-all-start = ((bf16[4,1,16,5,3072]{4,2,3,1,0:T(8,128)(2,1)}), bf16[4,1,16,5,3072]{4,2,3,1,0:T(8,128)(2,1)S(1)}, u32[]{:S(2)}, u32[]{:S(2)}) async-start(bf16[4,1,16,5,3072]{4,2,3,1,0:T(8,128)(2,1)} %copy.39), calls=%async_computation | async-start | bytes 3932160 | tf_op jit(solution)/shard_map/all_to_all | solution.py:13
Sparse Core Ops, SparseCore 0:
  12.5 88.1 all-reduce.1
